TPU v7x, 1024 devices: a whole 4x8x16 slice. The times are simulated.
1024 devices in a mesh: row: 32 (over z_lo, y), col: 32 (over x, z_hi, core).
Axes of the slice: x: 4, y: 8, z: 16 (z_hi: 4, z_lo: 4; z = z_hi * 4 + z_lo), core: 2. Of those that a mesh axis runs over, the one named last changes fastest.
Arguments:
- coeff: bfloat16 [12288, 12288], P('row', 'col'), may hold values from -6 to 6
- bank: bfloat16 [16, 384, 384], replicated, may hold values from -0.09375 to 0.09375
- alpha_tiles: int32 [32, 24], replicated, may hold values from 0 to 31
- alpha_blocks: int32 [32, 24], replicated, may hold values from 0 to 15
- alpha_count: int32 [32], replicated, may hold values from 2 to 24, as said below
- beta_tiles: int32 [32, 24], replicated, may hold values from 0 to 31
- beta_blocks: int32 [32, 24], replicated, may hold values from 0 to 15
- beta_count: int32 [32], replicated, may hold values from 2 to 24, as said below
Outputs:
- sigma: float32 [12288, 12288], P('row', 'col')
Inputs may be any that keep to these rules, and one draw needn't show every extreme that they name: `alpha_count`: every value lies in 2 to 24; some tile has all 24 slots live. `beta_count`: every value lies in 2 to 24; some tile has all 24 slots live.
All inputs are finite; a program needn't handle non-finite values.
Results may differ from a plain program's by a relative error of at most 0.0003.
Values may be sent and summed in bfloat16 or wider, within the bound.
No kernel may reach another device: no remote copies, remote signals or barrier semaphores. Data moves between devices by JAX's collectives and lax.ppermute only.
A program may use at most 64 MiB of HBM per device.

v0:
```python
import jax
import jax.numpy as jnp
from jax import lax
from jax.sharding import PartitionSpec as P


def left_apply(total, bank, block_id, piece):
    return total + jnp.dot(bank[block_id], piece, preferred_element_type=jnp.float32)


def right_apply(total, bank, block_id, piece):
    return total + lax.dot_general(
        piece, bank[block_id], (((1,), (1,)), ((), ())), preferred_element_type=jnp.float32
    )


def local(coeff, bank, alpha_tiles, alpha_blocks, alpha_count, beta_tiles, beta_blocks, beta_count):
    tile = coeff.shape[0]
    row_place = lax.axis_index("row")
    col_place = lax.axis_index("col")
    a_tiles = alpha_tiles[row_place]
    a_blocks = alpha_blocks[row_place]
    a_count = alpha_count[row_place]
    b_tiles = beta_tiles[col_place]
    b_blocks = beta_blocks[col_place]
    b_count = beta_count[col_place]
    zeros = jnp.zeros((tile, tile), jnp.float32)
    stacked = lax.all_gather(coeff, "row", axis=0, tiled=True)

    def add_alpha(slot, total):
        piece = lax.dynamic_slice_in_dim(stacked, a_tiles[slot] * tile, tile, 0)
        return left_apply(total, bank, a_blocks[slot], piece)

    sigma_alpha = lax.fori_loop(0, a_count, add_alpha, zeros)
    across = lax.all_gather(coeff, "col", axis=1, tiled=True)

    def add_beta(slot, total):
        piece = lax.dynamic_slice_in_dim(across, b_tiles[slot] * tile, tile, 1)
        return right_apply(total, bank, b_blocks[slot], piece)

    sigma_beta = lax.fori_loop(0, b_count, add_beta, zeros)
    return sigma_alpha + sigma_beta


def solution(mesh):
    return jax.shard_map(
        local,
        mesh=mesh,
        in_specs=(P("row", "col"), P(), P(), P(), P(), P(), P(), P()),
        out_specs=P("row", "col"),
        check_vma=False,
    )
```

profile of v0, /device:TPU:2, one launch (start us, length us, event | category | flops | bytes accessed | tf_op | source)
XLA Modules:
  0.0 501.7 jit_solution(17861045883723723662)
XLA Ops:
  12.3 171.0 %all-gather.5.cloned.1.call-done = bf16[384,12288]{1,0:T(8,128)(2,1)} async-done(((bf16[384,384]{1,0:T(8,128)(2,1)}), bf16[384,12288]{1,0:T(8,128)(2,1)}) %all-gather.5.cloned.1.call-update) | async-done | bytes 9437200 | tf_op jit(solution)/shard_map/all_gather | solution.py:35
  183.4 92.9 %while.21 = (s32[]{:T(128)}, f32[384,384]{1,0:T(8,128)S(1)}, s32[]{:T(128)}, s32[24]{0:T(128)S(1)}, bf16[384,12288]{1,0:T(8,128)(2,1)}, /*index=5*/s32[24]{0:T(1...) while((s32[]{:T(128)}, f32[384,384]{1,0:T(8,128)S(1)}, ...), condition=%wide.region_3.0_spmd, body=%wide.region_2.0_spmd.sunk | while | flops 113393672 | bytes 1769743 | solution.py:41
  187.7 1.5 convolution_add_fusion.5
  193.4 1.5 convolution_add_fusion.5
  199.2 1.5 convolution_add_fusion.5
  205.0 1.5 convolution_add_fusion.5
  210.7 1.5 convolution_add_fusion.5
  216.5 1.5 convolution_add_fusion.5
  222.3 1.5 convolution_add_fusion.5
  228.0 1.5 convolution_add_fusion.5
  233.8 1.5 convolution_add_fusion.5
  239.6 1.5 convolution_add_fusion.5
  245.4 1.5 convolution_add_fusion.5
  251.1 1.5 convolution_add_fusion.5
  256.9 1.5 convolution_add_fusion.5
  262.7 1.5 convolution_add_fusion.5
  268.4 1.5 convolution_add_fusion.5
  274.2 1.5 convolution_add_fusion.5
  276.3 76.0 %all-gather.3.cloned.1.call-done = bf16[12288,384]{1,0:T(8,128)(2,1)} async-done(((bf16[384,384]{1,0:T(8,128)(2,1)}), bf16[12288,384]{1,0:T(8,128)(2,1)}) %all-gather.3.cloned.1.call-update) | async-done | bytes 9437200 | tf_op jit(solution)/shard_map/all_gather | solution.py:28
  352.3 141.6 %while.20 = (s32[]{:T(128)}, f32[384,384]{1,0:T(8,128)S(1)}, s32[]{:T(128)}, s32[24]{0:T(128)S(1)}, bf16[16,384,384]{2,1,0:T(8,128)(2,1)}, /*index=5*/s32[24]{0:...) while((s32[]{:T(128)}, f32[384,384]{1,0:T(8,128)S(1)}, ...), condition=%wide.region_1.0_spmd, body=%wide.region_0.0_spmd.sunk | while | flops 113393672 | bytes 1769743 | solution.py:34
  356.7 1.4 convolution_add_fusion.4
  362.6 1.4 convolution_add_fusion.4
  368.5 1.4 convolution_add_fusion.4
  380.3 1.4 convolution_add_fusion.4
  (111 shorter events, 85.2 us)
Async XLA Ops:
  6.5 176.8 %all-gather.5.cloned.1.call-start = ((), (), s32[]{:S(2)}) async-start(), calls=%async_computation.1 | async-start | bytes 9732096 | tf_op jit(solution)/shard_map/all_gather | solution.py:35
  7.3 345.0 %all-gather.3.cloned.1.call-start = ((), (), s32[]{:S(2)}) async-start(), calls=%async_computation | async-start | bytes 9732096 | tf_op jit(solution)/shard_map/all_gather | solution.py:28
Sparse Core Ops, SparseCore 0:
  11.5 171.7 all-gather.4
  186.0 166.2 all-gather.2
where the time goes:
time: 505 us; the launch traced here: 502 us
  waiting for transfers between devices  248 us (49%)
  loops' own time  127 us (25%)
  matrix products  58 us (11%)
  local copies, waits for them, and re-layouts  54 us (11%)
  between operations  13.4 us (3%)
    all_gather x1, waiting for transfers between devices, local(): across = lax.all_gather(coeff, 'col', axis=1, tiled=True)  171 us
    another operation x1, loops' own time, local(): sigma_alpha = lax.fori_loop(0, a_count, add_alpha, zeros)  76.4 us
    all_gather x1, waiting for transfers between devices, local(): stacked = lax.all_gather(coeff, 'row', axis=0, tiled=True)  76 us
    another operation x1, loops' own time, local(): sigma_beta = lax.fori_loop(0, b_count, add_beta, zeros)  50.5 us
    dot_general x24, matrix products, left_apply(): jnp.dot(bank[block_id], piece, preferred_element_type=jnp.float32)  34.6 us
    dot_general x16, matrix products, right_apply(): lax.dot_general(piece, bank[block_id], (((1,), (1,)), ((), ())), preferre...  23.5 us
    dynamic_slice x24, local copies, waits for them, and re-layouts, add_alpha(): piece = lax.dynamic_slice_in_dim(stacked, a_tiles[slot] * tile, tile, 0)  15.3 us
    dynamic_slice x24, local copies, waits for them, and re-layouts, add_alpha(): return left_apply(total, bank, a_blocks[slot], piece)  15.3 us
  transfers between devices with their start and end apart: 2, of which 2 were waited for; matrix products, arithmetic and copies ran while one was open for 9% of the time, Pallas kernels for 0%

commit v1 on v0

v1 whole, which is shorter than its diff:
```python
import jax
import jax.numpy as jnp
from jax import lax
from jax.experimental import pallas as pl
from jax.experimental.pallas import tpu as pltpu
from jax.sharding import PartitionSpec as P

LANE = 128
PAD = 16
PAIR = 2
CHAINS = 2
ROOM = 24 << 20
VMEM = pl.BlockSpec(memory_space=pltpu.VMEM)
SMEM = pl.BlockSpec(memory_space=pltpu.SMEM)


def inside(x):
    return pltpu.with_memory_space_constraint(x, pltpu.VMEM)


def wire_rows(width, tile):
    return -(-(width * tile // LANE + 1) // 8) * 8


def pack_kernel(x_ref, out_ref, flip_ref, *, flip):
    parts, rows, _ = out_ref.shape
    tile = x_ref.shape[0]
    width = tile // parts
    used = width * tile // LANE
    x = x_ref[...]
    top = jnp.max(jnp.max(jnp.abs(x.astype(jnp.float32)), axis=0, keepdims=True), axis=1, keepdims=True)
    foot = jnp.broadcast_to(top, (rows - used, LANE)).astype(out_ref.dtype)
    if flip:
        flip_ref[...] = x.astype(jnp.float32).T.astype(x.dtype)
        src = flip_ref
    else:
        src = x_ref
    for t in range(parts):
        for block in range(tile // LANE):
            out_ref[t, block * width : (block + 1) * width, :] = src[
                t * width : (t + 1) * width, block * LANE : (block + 1) * LANE
            ]
        out_ref[t, used:, :] = foot


def pack(piece, parts, flip):
    tile = piece.shape[0]
    return pl.pallas_call(
        lambda *refs: pack_kernel(*refs, flip=flip),
        out_shape=jax.ShapeDtypeStruct((parts, wire_rows(tile // parts, tile), LANE), piece.dtype),
        in_specs=[VMEM],
        out_specs=VMEM,
        scratch_shapes=[pltpu.VMEM((tile, tile), piece.dtype)],
        compiler_params=pltpu.CompilerParams(vmem_limit_bytes=ROOM),
        name="pack_flip" if flip else "pack",
    )(piece)


def mix_kernel(places, cap, in_ref, bank_ref, out_ref, scale_ref, x_ref, prod_ref):
    banks, tile, _ = bank_ref.shape
    parts = in_ref.shape[0]
    width = tile // parts
    used = width * tile // LANE
    lanes = x_ref.shape[0]

    def unpack(t, top):
        x_ref[pl.ds(pl.multiple_of(t * PAD, PAD), PAD), :] = jnp.zeros((PAD, tile), x_ref.dtype)
        for block in range(tile // LANE):
            x_ref[pl.ds(pl.multiple_of(t * PAD, PAD), width), block * LANE : (block + 1) * LANE] = in_ref[
                t, block * width : (block + 1) * width, :
            ]
        return jnp.maximum(top, in_ref[t, used : used + 1, :].astype(jnp.float32))

    top = lax.fori_loop(0, parts, unpack, jnp.zeros((1, LANE), jnp.float32))
    scale = 32768.0 / jnp.maximum(top * cap[0], 1e-30)
    scale_ref[...] = 1.0 / scale
    prod_ref[pl.ds(banks * lanes, PAD), :] = jnp.zeros((PAD, tile), jnp.float32)

    for b in range(0, banks, PAIR):
        both = lax.dot_general(
            x_ref[...],
            bank_ref[b : b + PAIR].reshape(PAIR * tile, tile),
            (((1,), (1,)), ((), ())),
            preferred_element_type=jnp.float32,
        )
        for side in range(PAIR):
            prod_ref[pl.ds((b + side) * lanes, lanes), :] = both[:, side * tile : (side + 1) * tile]

    def gather(r, carry):
        totals = [None] * CHAINS
        for slot in range(places.shape[1]):
            piece = prod_ref[pl.ds(pl.multiple_of(places[r, slot], PAD), PAD), :]
            chain = slot % CHAINS
            totals[chain] = piece if totals[chain] is None else totals[chain] + piece
        total = sum(totals[1:], totals[0])
        for block in range(tile // LANE):
            out_ref[r, block * width : (block + 1) * width, :] = (
                total[:width, block * LANE : (block + 1) * LANE] * scale
            )
        return carry

    lax.fori_loop(0, parts, gather, 0)


def mix(pieces, bank, places, cap):
    parts, _, _ = pieces.shape
    banks, tile, _ = bank.shape
    out, unscale = pl.pallas_call(
        mix_kernel,
        out_shape=(
            jax.ShapeDtypeStruct((parts, tile // parts * tile // LANE, LANE), jnp.float32),
            jax.ShapeDtypeStruct((1, LANE), jnp.float32),
        ),
        in_specs=[SMEM, SMEM, VMEM, VMEM],
        out_specs=(VMEM, VMEM),
        scratch_shapes=[
            pltpu.VMEM((parts * PAD, tile), pieces.dtype),
            pltpu.VMEM((banks * parts * PAD + PAD, tile), jnp.float32),
        ],
        compiler_params=pltpu.CompilerParams(vmem_limit_bytes=ROOM),
        name="mix",
    )(places, cap, inside(pieces), bank)
    return out.astype(jnp.float16), unscale


def find(tiles, blocks, count, banks):
    rows, slots = tiles.shape
    at = blocks * (rows * PAD) + tiles * PAD
    return jnp.where(jnp.arange(slots) < count[:, None], at, banks * rows * PAD)


def join_kernel(alpha_ref, beta_ref, alpha_unit, beta_unit, out_ref, flip_ref):
    parts, _, _ = beta_ref.shape
    tile = out_ref.shape[0]
    width = tile // parts
    for t in range(parts):
        for block in range(tile // LANE):
            flip_ref[t * width : (t + 1) * width, block * LANE : (block + 1) * LANE] = alpha_ref[
                t, block * width : (block + 1) * width, :
            ]
    out_ref[...] = (flip_ref[...] * alpha_unit[0, 0]).T
    for t in range(parts):
        for block in range(tile // LANE):
            out_ref[t * width : (t + 1) * width, block * LANE : (block + 1) * LANE] += (
                beta_ref[t, block * width : (block + 1) * width, :] * beta_unit[0, 0]
            )


def join(alpha, beta, alpha_unit, beta_unit, tile):
    return pl.pallas_call(
        join_kernel,
        out_shape=jax.ShapeDtypeStruct((tile, tile), jnp.float32),
        in_specs=[VMEM, VMEM, SMEM, SMEM],
        out_specs=VMEM,
        scratch_shapes=[pltpu.VMEM((tile, tile), jnp.float32)],
        compiler_params=pltpu.CompilerParams(vmem_limit_bytes=ROOM),
        name="join",
    )(inside(alpha.astype(jnp.float32)), inside(beta.astype(jnp.float32)), alpha_unit, beta_unit)


def swap(pieces, axis):
    return lax.all_to_all(pieces, axis, 0, 0, tiled=True)


def local(coeff, bank, alpha_tiles, alpha_blocks, alpha_count, beta_tiles, beta_blocks, beta_count):
    tile = coeff.shape[0]
    banks = bank.shape[0]
    n_row = lax.axis_size("row")
    n_col = lax.axis_size("col")
    slots = alpha_tiles.shape[1]
    held = inside(bank)
    beta_in = swap(pack(coeff, n_col, False), "col")
    alpha_in = swap(pack(coeff, n_row, True), "row")
    cap = (jnp.max(jnp.abs(bank)).astype(jnp.float32) * (slots * tile)).reshape(1)
    alpha_at = find(alpha_tiles, alpha_blocks, alpha_count, banks)
    beta_at = find(beta_tiles, beta_blocks, beta_count, banks)
    alpha_mix, alpha_unit = mix(alpha_in, held, alpha_at, cap)
    alpha_out = swap(alpha_mix, "row")
    beta_mix, beta_unit = mix(beta_in, held, beta_at, cap)
    beta_out = swap(beta_mix, "col")
    return join(alpha_out, beta_out, alpha_unit, beta_unit, tile)


def solution(mesh):
    return jax.shard_map(
        local,
        mesh=mesh,
        in_specs=(P("row", "col"), P(), P(), P(), P(), P(), P(), P()),
        out_specs=P("row", "col"),
        check_vma=False,
    )
```

time: 505 us -> 131 us (0.26)
  the two profiles are of different devices: /device:TPU:2 before, /device:TPU:8 now
where the time goes in v1:
time: 131 us; the launch traced here: 130 us
  starting transfers between devices  56.8 us (43%)
  waiting for transfers between devices  44 us (34%)
  Pallas kernels  15 us (11%)
  local copies, waits for them, and re-layouts  8.32 us (6%)
  other arithmetic  5.42 us (4%)
    all_to_all x4, starting transfers between devices, swap(): return lax.all_to_all(pieces, axis, 0, 0, tiled=True)  56.8 us
    all_to_all x4, waiting for transfers between devices, swap(): return lax.all_to_all(pieces, axis, 0, 0, tiled=True)  44 us
    pallas_call x2, Pallas kernels, mix(): pl.pallas_call(mix_kernel, out_shape=(jax.ShapeDtypeStruct((parts, tile /...  11.6 us
    unnamed x20, local copies, waits for them, and re-layouts  8.32 us
    reduce_max x1, other arithmetic, local(): jnp.max(jnp.abs(bank)).astype(jnp.float32) * (slots * tile)  3.65 us
  transfers between devices with their start and end apart: 4, of which 3 were waited for; matrix products, arithmetic and copies ran while one was open for 5% of the time, Pallas kernels for 10%

profile of v1, /device:TPU:8, one launch (start us, length us, event | category | flops | bytes accessed | tf_op | source)
XLA Modules:
  0.0 130.3 jit_solution(7448833915971416811)
XLA Ops:
  0.0 1.0 copy-done.2
  1.0 0.8 pack.1
  1.8 21.6 %all-to-all-start.2 = ((bf16[32,40,128]{2,1,0:T(8,128)(2,1)}), bf16[32,40,128]{2,1,0:T(8,128)(2,1)S(1)}, u32[]{:S(2)}, u32[]{:S(2)}) async-start(bf16[32,40,128]{2,1,0:T(8,128)(2,1)} %pack.1), calls=%async_computation.2 | async-start | bytes 655360 | tf_op jit(solution)/shard_map/all_to_all | solution.py:162
  23.4 1.0 copy-done.3
  24.4 1.0 pack_flip.1
  25.3 19.4 %all-to-all-done.2.in_ref = bf16[32,40,128]{2,1,0:T(8,128)(2,1)S(1)} async-done(((bf16[32,40,128]{2,1,0:T(8,128)(2,1)}), bf16[32,40,128]{2,1,0:T(8,128)(2,1)S(1)}, u32[]{:S(2)}, u32[]{:S(2)}) %all-to-all-start.2) | async-done | bytes 327712 | tf_op jit(solution)/shard_map/all_to_all | solution.py:162
  44.8 15.8 %all-to-all-start = ((bf16[32,40,128]{2,1,0:T(8,128)(2,1)}), bf16[32,40,128]{2,1,0:T(8,128)(2,1)S(1)}, u32[]{:S(2)}, u32[]{:S(2)}) async-start(bf16[32,40,128]{2,1,0:T(8,128)(2,1)} %pack_flip.1), calls=%async_computation | async-start | bytes 655360 | tf_op jit(solution)/shard_map/all_to_all | solution.py:162
  60.6 0.8 copy.12
  61.4 0.8 copy.11
  62.2 3.7 %abs_reduce_fusion = bf16[]{:T(256)} fusion(bf16[16,384,384]{2,1,0:T(8,128)(2,1)} %bank_ref.3), kind=kLoop, calls=%fused_computation | loop fusion | flops 4718591 | bytes 4718594 | tf_op jit(solution)/shard_map/reduce_max | solution.py:174
  66.5 0.1 add_select_fusion.places
  66.6 2.3 %copy-done = bf16[16,384,384]{2,1,0:T(8,128)(2,1)S(1)} copy-done((bf16[16,384,384]{2,1,0:T(8,128)(2,1)S(1)}, bf16[16,384,384]{2,1,0:T(8,128)(2,1)}, u32[]{:S(2)}) %copy-start) | copy-done | bytes 4718616
  68.9 5.8 %mix.3 = (f32[32,36,128]{2,1,0:T(8,128)S(1)}, f32[1,128]{1,0:T(1,128)S(1)}) custom-call(s32[32,24]{1,0:T(8,128)S(1)} %add_select_fusion.places, f32[1]{0:T(128)} %bitcast.cap, bf16[32,40,128]{2,1,0:T(8,128)(2,1)S(1)} %all-to-all-done.2.in_ref, bf16[16,384,384]{2,1,0:T(8,128)(2,1)S(1)} %copy-done), custom_call_target="tpu_custom_call" | custom-call | tf_op jit(solution)/shard_map/mix/pallas_call | solution.py:108
  74.7 0.8 convert_element_type.18
  75.4 3.9 %all-to-all-start.3 = ((f16[32,36,128]{2,1,0:T(8,128)(2,1)}), f16[32,36,128]{2,1,0:T(8,128)(2,1)S(1)}, u32[]{:S(2)}, u32[]{:S(2)}) async-start(f16[32,36,128]{2,1,0:T(8,128)(2,1)} %convert_element_type.18), calls=%async_computation.3 | async-start | bytes 655360 | tf_op jit(solution)/shard_map/all_to_all | solution.py:162
  79.3 0.1 copy.10
  79.5 0.1 add_select_fusion.1.places
  79.6 2.3 %copy-done.1 = bf16[16,384,384]{2,1,0:T(8,128)(2,1)S(1)} copy-done((bf16[16,384,384]{2,1,0:T(8,128)(2,1)S(1)}, bf16[16,384,384]{2,1,0:T(8,128)(2,1)}, u32[]{:S(2)}) %copy-start.1) | copy-done | bytes 4718616
  81.9 5.8 %mix.2 = (f32[32,36,128]{2,1,0:T(8,128)S(1)}, f32[1,128]{1,0:T(1,128)S(1)}) custom-call(s32[32,24]{1,0:T(8,128)S(1)} %add_select_fusion.1.places, f32[1]{0:T(128)} %bitcast.cap, bf16[32,40,128]{2,1,0:T(8,128)(2,1)S(1)} %all-to-all-done.in_ref, bf16[16,384,384]{2,1,0:T(8,128)(2,1)S(1)} %copy-done.1), custom_call_target="tpu_custom_call" | custom-call | tf_op jit(solution)/shard_map/mix/pallas_call | solution.py:108
  87.7 0.8 convert_element_type.16
  88.5 12.2 %all-to-all-done.3 = f16[32,36,128]{2,1,0:T(8,128)(2,1)S(1)} async-done(((f16[32,36,128]{2,1,0:T(8,128)(2,1)}), f16[32,36,128]{2,1,0:T(8,128)(2,1)S(1)}, u32[]{:S(2)}, u32[]{:S(2)}) %all-to-all-start.3) | async-done | bytes 294944 | tf_op jit(solution)/shard_map/all_to_all | solution.py:162
  100.7 15.5 %all-to-all-start.1 = ((f16[32,36,128]{2,1,0:T(8,128)(2,1)}), f16[32,36,128]{2,1,0:T(8,128)(2,1)S(1)}, u32[]{:S(2)}, u32[]{:S(2)}) async-start(f16[32,36,128]{2,1,0:T(8,128)(2,1)} %convert_element_type.16), calls=%async_computation.1 | async-start | bytes 655360 | tf_op jit(solution)/shard_map/all_to_all | solution.py:162
  116.3 12.3 %all-to-all-done.1 = f16[32,36,128]{2,1,0:T(8,128)(2,1)S(1)} async-done(((f16[32,36,128]{2,1,0:T(8,128)(2,1)}), f16[32,36,128]{2,1,0:T(8,128)(2,1)S(1)}, u32[]{:S(2)}, u32[]{:S(2)}) %all-to-all-start.1) | async-done | bytes 294944 | tf_op jit(solution)/shard_map/all_to_all | solution.py:162
  128.6 1.7 %join.1 = f32[384,384]{1,0:T(8,128)} custom-call(f32[32,36,128]{2,1,0:T(8,128)S(1)} %convert_element_type.17.alpha_ref, f32[32,36,128]{2,1,0:T(8,128)S(1)} %convert_element_type.19.beta_ref, f32[1,128]{1,0:T(1,128)S(1)} %get-tuple-element.11.alpha_unit, f32[1,128]{1,0:T(1,128)S(1)} %get-tuple-element.12.beta_unit), custom_call_target="tpu_custom_call" | custom-call | tf_op jit(solution)/shard_map/join/pallas_call | solution.py:150
  (16 shorter events, 0.2 us)
Async XLA Ops:
  0.0 1.0 copy-start.2
  1.0 65.5 %copy-start.6 = (s32[32]{0:T(128)S(1)}, s32[32]{0:T(128)}, u32[]{:S(2)}) copy-start(s32[32]{0:T(128)} %param.15) | copy-start | bytes 388
  1.8 43.0 %all-to-all-start.2 = ((bf16[32,40,128]{2,1,0:T(8,128)(2,1)}), bf16[32,40,128]{2,1,0:T(8,128)(2,1)S(1)}, u32[]{:S(2)}, u32[]{:S(2)}) async-start(bf16[32,40,128]{2,1,0:T(8,128)(2,1)} %pack.1), calls=%async_computation.2 | async-start | bytes 655360 | tf_op jit(solution)/shard_map/all_to_all | solution.py:162
  23.4 1.0 copy-start.3
  44.8 30.7 %all-to-all-start = ((bf16[32,40,128]{2,1,0:T(8,128)(2,1)}), bf16[32,40,128]{2,1,0:T(8,128)(2,1)S(1)}, u32[]{:S(2)}, u32[]{:S(2)}) async-start(bf16[32,40,128]{2,1,0:T(8,128)(2,1)} %pack_flip.1), calls=%async_computation | async-start | bytes 655360 | tf_op jit(solution)/shard_map/all_to_all | solution.py:162
  62.2 17.2 %copy-start.4 = (s32[32,24]{0,1:T(8,128)S(1)}, s32[32,24]{0,1:T(8,128)}, u32[]{:S(2)}) copy-start(s32[32,24]{0,1:T(8,128)} %param.10) | copy-start | bytes 9220
  62.2 17.2 %copy-start.5 = (s32[32,24]{0,1:T(8,128)S(1)}, s32[32,24]{0,1:T(8,128)}, u32[]{:S(2)}) copy-start(s32[32,24]{0,1:T(8,128)} %param.11) | copy-start | bytes 9220
  62.2 17.3 %copy-start.7 = (s32[32]{0:T(128)S(1)}, s32[32]{0:T(128)}, u32[]{:S(2)}) copy-start(s32[32]{0:T(128)} %param.12) | copy-start | bytes 388
  66.6 2.3 %copy-start = (bf16[16,384,384]{2,1,0:T(8,128)(2,1)S(1)}, bf16[16,384,384]{2,1,0:T(8,128)(2,1)}, u32[]{:S(2)}) copy-start(bf16[16,384,384]{2,1,0:T(8,128)(2,1)} %bank_ref.3) | copy-start | bytes 14155780
  75.4 25.3 %all-to-all-start.3 = ((f16[32,36,128]{2,1,0:T(8,128)(2,1)}), f16[32,36,128]{2,1,0:T(8,128)(2,1)S(1)}, u32[]{:S(2)}, u32[]{:S(2)}) async-start(f16[32,36,128]{2,1,0:T(8,128)(2,1)} %convert_element_type.18), calls=%async_computation.3 | async-start | bytes 655360 | tf_op jit(solution)/shard_map/all_to_all | solution.py:162
  79.6 2.3 %copy-start.1 = (bf16[16,384,384]{2,1,0:T(8,128)(2,1)S(1)}, bf16[16,384,384]{2,1,0:T(8,128)(2,1)}, u32[]{:S(2)}) copy-start(bf16[16,384,384]{2,1,0:T(8,128)(2,1)} %bank_ref.3) | copy-start | bytes 14155780
  100.7 27.9 %all-to-all-start.1 = ((f16[32,36,128]{2,1,0:T(8,128)(2,1)}), f16[32,36,128]{2,1,0:T(8,128)(2,1)S(1)}, u32[]{:S(2)}, u32[]{:S(2)}) async-start(f16[32,36,128]{2,1,0:T(8,128)(2,1)} %convert_element_type.16), calls=%async_computation.1 | async-start | bytes 655360 | tf_op jit(solution)/shard_map/all_to_all | solution.py:162

commit v2 on v1

--- a/solution.py
+++ b/solution.py
@@ -56,12 +56,19 @@
     )(piece)
 
 
-def mix_kernel(places, cap, in_ref, bank_ref, out_ref, scale_ref, x_ref, prod_ref):
+def mix_kernel(places, cap, in_ref, bank_hbm, out_ref, scale_ref, x_ref, prod_ref, bank_ref, sems):
     banks, tile, _ = bank_ref.shape
     parts = in_ref.shape[0]
     width = tile // parts
     used = width * tile // LANE
     lanes = x_ref.shape[0]
+    edges = [0, PAIR, banks // 2, banks]
+    copies = {
+        low: pltpu.make_async_copy(bank_hbm.at[pl.ds(low, high - low)], bank_ref.at[pl.ds(low, high - low)], sems.at[i])
+        for i, (low, high) in enumerate(zip(edges[:-1], edges[1:]))
+    }
+    for copy in copies.values():
+        copy.start()
 
     def unpack(t, top):
         x_ref[pl.ds(pl.multiple_of(t * PAD, PAD), PAD), :] = jnp.zeros((PAD, tile), x_ref.dtype)
@@ -77,6 +84,8 @@
     prod_ref[pl.ds(banks * lanes, PAD), :] = jnp.zeros((PAD, tile), jnp.float32)
 
     for b in range(0, banks, PAIR):
+        if b in copies:
+            copies[b].wait()
         both = lax.dot_general(
             x_ref[...],
             bank_ref[b : b + PAIR].reshape(PAIR * tile, tile),
@@ -111,15 +120,17 @@
             jax.ShapeDtypeStruct((parts, tile // parts * tile // LANE, LANE), jnp.float32),
             jax.ShapeDtypeStruct((1, LANE), jnp.float32),
         ),
-        in_specs=[SMEM, SMEM, VMEM, VMEM],
+        in_specs=[SMEM, SMEM, VMEM, pl.BlockSpec(memory_space=pltpu.HBM)],
         out_specs=(VMEM, VMEM),
         scratch_shapes=[
             pltpu.VMEM((parts * PAD, tile), pieces.dtype),
             pltpu.VMEM((banks * parts * PAD + PAD, tile), jnp.float32),
+            pltpu.VMEM(bank.shape, bank.dtype),
+            pltpu.SemaphoreType.DMA((3,)),
         ],
         compiler_params=pltpu.CompilerParams(vmem_limit_bytes=ROOM),
         name="mix",
-    )(places, cap, inside(pieces), bank)
+    )(places, cap, inside(pieces), pltpu.with_memory_space_constraint(bank, pltpu.HBM))
     return out.astype(jnp.float16), unscale
 
 
@@ -129,33 +140,49 @@
     return jnp.where(jnp.arange(slots) < count[:, None], at, banks * rows * PAD)
 
 
-def join_kernel(alpha_ref, beta_ref, alpha_unit, beta_unit, out_ref, flip_ref):
-    parts, _, _ = beta_ref.shape
+def turn_kernel(parts_ref, unit, out_ref, flip_ref):
+    parts = parts_ref.shape[0]
     tile = out_ref.shape[0]
     width = tile // parts
     for t in range(parts):
         for block in range(tile // LANE):
-            flip_ref[t * width : (t + 1) * width, block * LANE : (block + 1) * LANE] = alpha_ref[
+            flip_ref[t * width : (t + 1) * width, block * LANE : (block + 1) * LANE] = parts_ref[
                 t, block * width : (block + 1) * width, :
             ]
-    out_ref[...] = (flip_ref[...] * alpha_unit[0, 0]).T
+    out_ref[...] = flip_ref[...].T * unit[0, 0]
+
+
+def turn(parts, unit, tile):
+    return pl.pallas_call(
+        turn_kernel,
+        out_shape=jax.ShapeDtypeStruct((tile, tile), jnp.float32),
+        in_specs=[VMEM, SMEM],
+        out_specs=VMEM,
+        scratch_shapes=[pltpu.VMEM((tile, tile), jnp.float32)],
+        compiler_params=pltpu.CompilerParams(vmem_limit_bytes=ROOM),
+        name="turn",
+    )(inside(parts.astype(jnp.float32)), unit)
+
+
+def join_kernel(base_ref, parts_ref, unit, out_ref):
+    parts = parts_ref.shape[0]
+    tile = out_ref.shape[0]
+    width = tile // parts
     for t in range(parts):
         for block in range(tile // LANE):
-            out_ref[t * width : (t + 1) * width, block * LANE : (block + 1) * LANE] += (
-                beta_ref[t, block * width : (block + 1) * width, :] * beta_unit[0, 0]
-            )
-
-
-def join(alpha, beta, alpha_unit, beta_unit, tile):
+            rows, cols = slice(t * width, (t + 1) * width), slice(block * LANE, (block + 1) * LANE)
+            out_ref[rows, cols] = base_ref[rows, cols] + parts_ref[t, block * width : (block + 1) * width, :] * unit[0, 0]
+
+
+def join(base, parts, unit):
     return pl.pallas_call(
         join_kernel,
-        out_shape=jax.ShapeDtypeStruct((tile, tile), jnp.float32),
-        in_specs=[VMEM, VMEM, SMEM, SMEM],
+        out_shape=jax.ShapeDtypeStruct(base.shape, jnp.float32),
+        in_specs=[VMEM, VMEM, SMEM],
         out_specs=VMEM,
-        scratch_shapes=[pltpu.VMEM((tile, tile), jnp.float32)],
         compiler_params=pltpu.CompilerParams(vmem_limit_bytes=ROOM),
         name="join",
-    )(inside(alpha.astype(jnp.float32)), inside(beta.astype(jnp.float32)), alpha_unit, beta_unit)
+    )(inside(base), inside(parts.astype(jnp.float32)), unit)
 
 
 def swap(pieces, axis):
@@ -168,17 +195,17 @@
     n_row = lax.axis_size("row")
     n_col = lax.axis_size("col")
     slots = alpha_tiles.shape[1]
-    held = inside(bank)
+    alpha_in = swap(pack(coeff, n_row, True), "row")
     beta_in = swap(pack(coeff, n_col, False), "col")
-    alpha_in = swap(pack(coeff, n_row, True), "row")
     cap = (jnp.max(jnp.abs(bank)).astype(jnp.float32) * (slots * tile)).reshape(1)
     alpha_at = find(alpha_tiles, alpha_blocks, alpha_count, banks)
     beta_at = find(beta_tiles, beta_blocks, beta_count, banks)
-    alpha_mix, alpha_unit = mix(alpha_in, held, alpha_at, cap)
+    alpha_mix, alpha_unit = mix(alpha_in, bank, alpha_at, cap)
+    beta_mix, beta_unit = mix(beta_in, bank, beta_at, cap)
     alpha_out = swap(alpha_mix, "row")
-    beta_mix, beta_unit = mix(beta_in, held, beta_at, cap)
     beta_out = swap(beta_mix, "col")
-    return join(alpha_out, beta_out, alpha_unit, beta_unit, tile)
+    base = turn(alpha_out, alpha_unit, tile)
+    return join(base, beta_out, beta_unit)
 
 
 def solution(mesh):

time: 131 us -> 124 us (0.947)
  the two profiles are of different devices: /device:TPU:8 before, /device:TPU:65 now
where the time goes in v2:
time: 124 us; the launch traced here: 123 us
  waiting for transfers between devices  47.6 us (38%)
  starting transfers between devices  46.9 us (38%)
  Pallas kernels  18.7 us (15%)
  other arithmetic  5.36 us (4%)
  local copies, waits for them, and re-layouts  3.64 us (3%)
    all_to_all x4, waiting for transfers between devices, swap(): return lax.all_to_all(pieces, axis, 0, 0, tiled=True)  47.6 us
    all_to_all x4, starting transfers between devices, swap(): return lax.all_to_all(pieces, axis, 0, 0, tiled=True)  46.9 us
    pallas_call x2, Pallas kernels, mix(): pl.pallas_call(mix_kernel, out_shape=(jax.ShapeDtypeStruct((parts, tile /...  14.6 us
    unnamed x16, local copies, waits for them, and re-layouts  3.64 us
    reduce_max x1, other arithmetic, local(): jnp.max(jnp.abs(bank)).astype(jnp.float32) * (slots * tile)  3.59 us
  transfers between devices with their start and end apart: 4, of which 4 were waited for; matrix products, arithmetic and copies ran while one was open for 6% of the time, Pallas kernels for 13%

profile of v2, /device:TPU:65, one launch (start us, length us, event | category | flops | bytes accessed | tf_op | source)
XLA Modules:
  0.0 123.0 jit_solution(4873920765635414707)
XLA Ops:
  0.0 1.0 copy-done
  1.0 1.0 pack_flip.1
  1.9 11.8 %all-to-all-start = ((bf16[32,40,128]{2,1,0:T(8,128)(2,1)}), bf16[32,40,128]{2,1,0:T(8,128)(2,1)S(1)}, u32[]{:S(2)}, u32[]{:S(2)}) async-start(bf16[32,40,128]{2,1,0:T(8,128)(2,1)} %pack_flip.1), calls=%async_computation | async-start | bytes 655360 | tf_op jit(solution)/shard_map/all_to_all | solution.py:189
  13.7 1.0 copy-done.1
  14.7 0.8 pack.1
  15.5 7.4 %all-to-all-done.in_ref = bf16[32,40,128]{2,1,0:T(8,128)(2,1)S(1)} async-done(((bf16[32,40,128]{2,1,0:T(8,128)(2,1)}), bf16[32,40,128]{2,1,0:T(8,128)(2,1)S(1)}, u32[]{:S(2)}, u32[]{:S(2)}) %all-to-all-start) | async-done | bytes 327712 | tf_op jit(solution)/shard_map/all_to_all | solution.py:189
  22.9 23.4 %all-to-all-start.2 = ((bf16[32,40,128]{2,1,0:T(8,128)(2,1)}), bf16[32,40,128]{2,1,0:T(8,128)(2,1)S(1)}, u32[]{:S(2)}, u32[]{:S(2)}) async-start(bf16[32,40,128]{2,1,0:T(8,128)(2,1)} %pack.1), calls=%async_computation.2 | async-start | bytes 655360 | tf_op jit(solution)/shard_map/all_to_all | solution.py:189
  46.4 0.8 copy.10
  47.2 0.8 copy.9
  48.0 3.6 %abs_reduce_fusion = bf16[]{:T(256)} fusion(bf16[16,384,384]{2,1,0:T(8,128)(2,1)} %bank_hbm.3), kind=kLoop, calls=%fused_computation | loop fusion | flops 4718591 | bytes 4718594 | tf_op jit(solution)/shard_map/reduce_max | solution.py:200
  52.2 0.1 add_select_fusion.1.places
  52.3 7.3 %mix.2 = (f32[32,36,128]{2,1,0:T(8,128)S(1)}, f32[1,128]{1,0:T(1,128)S(1)}) custom-call(s32[32,24]{1,0:T(8,128)S(1)} %add_select_fusion.1.places, f32[1]{0:T(128)} %bitcast.cap, bf16[32,40,128]{2,1,0:T(8,128)(2,1)S(1)} %all-to-all-done.in_ref, bf16[16,384,384]{2,1,0:T(8,128)(2,1)} %bank_hbm.3), custom_call_target="tpu_custom_call" | custom-call | tf_op jit(solution)/shard_map/mix/pallas_call | solution.py:117
  59.6 0.8 convert_element_type.16
  60.4 12.7 %all-to-all-done.2.in_ref = bf16[32,40,128]{2,1,0:T(8,128)(2,1)S(1)} async-done(((bf16[32,40,128]{2,1,0:T(8,128)(2,1)}), bf16[32,40,128]{2,1,0:T(8,128)(2,1)S(1)}, u32[]{:S(2)}, u32[]{:S(2)}) %all-to-all-start.2) | async-done | bytes 327712 | tf_op jit(solution)/shard_map/all_to_all | solution.py:189
  73.0 4.1 %all-to-all-start.1 = ((f16[32,36,128]{2,1,0:T(8,128)(2,1)}), f16[32,36,128]{2,1,0:T(8,128)(2,1)S(1)}, u32[]{:S(2)}, u32[]{:S(2)}) async-start(f16[32,36,128]{2,1,0:T(8,128)(2,1)} %convert_element_type.16), calls=%async_computation.1 | async-start | bytes 655360 | tf_op jit(solution)/shard_map/all_to_all | solution.py:189
  77.2 0.1 copy.11
  77.3 0.1 add_select_fusion.places
  77.4 7.3 %mix.3 = (f32[32,36,128]{2,1,0:T(8,128)S(1)}, f32[1,128]{1,0:T(1,128)S(1)}) custom-call(s32[32,24]{1,0:T(8,128)S(1)} %add_select_fusion.places, f32[1]{0:T(128)} %bitcast.cap, bf16[32,40,128]{2,1,0:T(8,128)(2,1)S(1)} %all-to-all-done.2.in_ref, bf16[16,384,384]{2,1,0:T(8,128)(2,1)} %bank_hbm.3), custom_call_target="tpu_custom_call" | custom-call | tf_op jit(solution)/shard_map/mix/pallas_call | solution.py:117
  84.7 0.8 convert_element_type.18
  85.5 1.6 %all-to-all-done.1 = f16[32,36,128]{2,1,0:T(8,128)(2,1)S(1)} async-done(((f16[32,36,128]{2,1,0:T(8,128)(2,1)}), f16[32,36,128]{2,1,0:T(8,128)(2,1)S(1)}, u32[]{:S(2)}, u32[]{:S(2)}) %all-to-all-start.1) | async-done | bytes 294944 | tf_op jit(solution)/shard_map/all_to_all | solution.py:189
  87.0 7.7 %all-to-all-start.3 = ((f16[32,36,128]{2,1,0:T(8,128)(2,1)}), f16[32,36,128]{2,1,0:T(8,128)(2,1)S(1)}, u32[]{:S(2)}, u32[]{:S(2)}) async-start(f16[32,36,128]{2,1,0:T(8,128)(2,1)} %convert_element_type.18), calls=%async_computation.3 | async-start | bytes 655360 | tf_op jit(solution)/shard_map/all_to_all | solution.py:189
  94.7 0.8 turn.1.base_ref
  95.5 25.9 %all-to-all-done.3 = f16[32,36,128]{2,1,0:T(8,128)(2,1)S(1)} async-done(((f16[32,36,128]{2,1,0:T(8,128)(2,1)}), f16[32,36,128]{2,1,0:T(8,128)(2,1)S(1)}, u32[]{:S(2)}, u32[]{:S(2)}) %all-to-all-start.3) | async-done | bytes 294944 | tf_op jit(solution)/shard_map/all_to_all | solution.py:189
  121.5 1.5 %join.1 = f32[384,384]{1,0:T(8,128)} custom-call(f32[384,384]{1,0:T(8,128)S(1)} %turn.1.base_ref, f32[32,36,128]{2,1,0:T(8,128)S(1)} %convert_element_type.19.parts_ref, f32[1,128]{1,0:T(1,128)S(1)} %get-tuple-element.12.unit), custom_call_target="tpu_custom_call" | custom-call | tf_op jit(solution)/shard_map/join/pallas_call | solution.py:178
  (13 shorter events, 0.2 us)
Async XLA Ops:
  0.0 1.0 copy-start
  1.0 51.2 %copy-start.4 = (s32[32]{0:T(128)S(1)}, s32[32]{0:T(128)}, u32[]{:S(2)}) copy-start(s32[32]{0:T(128)} %param.12) | copy-start | bytes 388
  1.9 21.0 %all-to-all-start = ((bf16[32,40,128]{2,1,0:T(8,128)(2,1)}), bf16[32,40,128]{2,1,0:T(8,128)(2,1)S(1)}, u32[]{:S(2)}, u32[]{:S(2)}) async-start(bf16[32,40,128]{2,1,0:T(8,128)(2,1)} %pack_flip.1), calls=%async_computation | async-start | bytes 655360 | tf_op jit(solution)/shard_map/all_to_all | solution.py:189
  13.7 1.0 copy-start.1
  22.9 50.1 %all-to-all-start.2 = ((bf16[32,40,128]{2,1,0:T(8,128)(2,1)}), bf16[32,40,128]{2,1,0:T(8,128)(2,1)S(1)}, u32[]{:S(2)}, u32[]{:S(2)}) async-start(bf16[32,40,128]{2,1,0:T(8,128)(2,1)} %pack.1), calls=%async_computation.2 | async-start | bytes 655360 | tf_op jit(solution)/shard_map/all_to_all | solution.py:189
  47.9 29.2 %copy-start.2 = (s32[32,24]{0,1:T(8,128)S(1)}, s32[32,24]{0,1:T(8,128)}, u32[]{:S(2)}) copy-start(s32[32,24]{0,1:T(8,128)} %param.14) | copy-start | bytes 9220
  47.9 29.3 %copy-start.3 = (s32[32,24]{0,1:T(8,128)S(1)}, s32[32,24]{0,1:T(8,128)}, u32[]{:S(2)}) copy-start(s32[32,24]{0,1:T(8,128)} %param.13) | copy-start | bytes 9220
  47.9 29.4 %copy-start.5 = (s32[32]{0:T(128)S(1)}, s32[32]{0:T(128)}, u32[]{:S(2)}) copy-start(s32[32]{0:T(128)} %param.15) | copy-start | bytes 388
  73.0 14.0 %all-to-all-start.1 = ((f16[32,36,128]{2,1,0:T(8,128)(2,1)}), f16[32,36,128]{2,1,0:T(8,128)(2,1)S(1)}, u32[]{:S(2)}, u32[]{:S(2)}) async-start(f16[32,36,128]{2,1,0:T(8,128)(2,1)} %convert_element_type.16), calls=%async_computation.1 | async-start | bytes 655360 | tf_op jit(solution)/shard_map/all_to_all | solution.py:189
  87.0 34.4 %all-to-all-start.3 = ((f16[32,36,128]{2,1,0:T(8,128)(2,1)}), f16[32,36,128]{2,1,0:T(8,128)(2,1)S(1)}, u32[]{:S(2)}, u32[]{:S(2)}) async-start(f16[32,36,128]{2,1,0:T(8,128)(2,1)} %convert_element_type.18), calls=%async_computation.3 | async-start | bytes 655360 | tf_op jit(solution)/shard_map/all_to_all | solution.py:189
